TPU v7x, 256 devices: a whole 4x4x8 slice. The times are simulated.
256 devices in a mesh: grp: 4 (over z_hi), col: 16 (over y, z_lo, core), lay: 4 (over x).
Axes of the slice: x: 4, y: 4, z: 8 (z_hi: 4, z_lo: 2; z = z_hi * 2 + z_lo), core: 2. Of those that a mesh axis runs over, the one named last changes fastest.
Arguments:
- salinity: float32 [16, 1024, 2048], P('lay', ('grp', 'col')), may hold values from 0.3 to 4.2
- zone_ids: int32 [16, 1024, 2048], P('lay', ('grp', 'col')), may hold values from 0 to 7
- flow_speed: float32 [16, 1024, 2048], P('lay', ('grp', 'col')), may hold values from 0.5 to 4
- fixed_cells: int32 [16, 1024, 2048], P('lay', ('grp', 'col')), may hold values 0 or 1
- dispersivity: float32 [2, 8], replicated, may hold values from 50 to 1000
Outputs:
- salinity_next: float32 [16, 1024, 2048], P('lay', 'grp', 'col')
All inputs are finite; a program needn't handle non-finite values. No bound on the sum of `fixed_cells` on one device may be relied on, other than what follows from the above.
Results may differ from a plain program's by a relative error of at most 0.00005.
Values sent between devices are 32-bit elements; how exact they have to be, the bound alone decides.
A program may use at most 128 MiB of HBM per device.

v0:
```python
import jax
import jax.numpy as jnp
from jax import lax
from jax.sharding import PartitionSpec as P


def shifted(values, stride, line_axis, filler, heading):
    line_axis = line_axis % values.ndim
    length = values.shape[line_axis]
    edge_shape = list(values.shape)
    edge_shape[line_axis] = length
    padding = jnp.full(tuple(edge_shape), filler, values.dtype)
    padded = jnp.concatenate([padding, values, padding], axis=line_axis)
    return lax.dynamic_slice_in_dim(padded, length + heading * stride, length, axis=line_axis)


def reduce_lines(below_coef, middle, above_coef, right_side, line_axis):
    length = middle.shape[line_axis]
    levels = max(1, (length - 1).bit_length())

    def one_level(_, carry):
        below_now, middle_now, above_now, right_now, stride = carry
        weight_below = -below_now / shifted(middle_now, stride, line_axis, 1.0, -1)
        weight_above = -above_now / shifted(middle_now, stride, line_axis, 1.0, 1)
        below_next = weight_below * shifted(below_now, stride, line_axis, 0.0, -1)
        above_next = weight_above * shifted(above_now, stride, line_axis, 0.0, 1)
        middle_next = (
            middle_now
            + weight_below * shifted(above_now, stride, line_axis, 0.0, -1)
            + weight_above * shifted(below_now, stride, line_axis, 0.0, 1)
        )
        right_next = (
            right_now
            + weight_below * shifted(right_now, stride, line_axis, 0.0, -1)
            + weight_above * shifted(right_now, stride, line_axis, 0.0, 1)
        )
        return (below_next, middle_next, above_next, right_next, stride * 2)

    result = lax.fori_loop(
        0, levels, one_level, (below_coef, middle, above_coef, right_side, jnp.int32(1))
    )
    return result[3] / result[1]


def line_solve(coupling, field, line_axis):
    return reduce_lines(-coupling, 1.0 + 2.0 * coupling, -coupling, field, line_axis - field.ndim)


def couplings(zone_ids, flow_speed, fixed_cells, dispersivity):
    opened = 1.0 - fixed_cells.astype(jnp.float32)
    longit = jnp.zeros(flow_speed.shape, jnp.float32)
    transv = jnp.zeros(flow_speed.shape, jnp.float32)
    for number in range(dispersivity.shape[1]):
        matched = zone_ids == number
        longit = jnp.where(matched, dispersivity[0, number], longit)
        transv = jnp.where(matched, dispersivity[1, number], transv)
    return (opened * longit * flow_speed, opened * transv * flow_speed)


def block_parts(field, coupling, line_axis):
    length = field.shape[line_axis]
    places = lax.broadcasted_iota(jnp.int32, field.shape, line_axis)
    firsts = (places == 0).astype(jnp.float32)
    lasts = (places == length - 1).astype(jnp.float32)
    stacked = jnp.stack([field, firsts, lasts])
    solved = reduce_lines(
        -coupling, 1.0 + 2.0 * coupling, -coupling, stacked, line_axis - field.ndim
    )
    interior = solved[0]
    weight_low = lax.index_in_dim(coupling, 0, line_axis, keepdims=True) * solved[1]
    weight_high = lax.index_in_dim(coupling, length - 1, line_axis, keepdims=True) * solved[2]
    edges = jnp.stack(
        [
            lax.index_in_dim(interior, 0, line_axis, keepdims=False),
            lax.index_in_dim(interior, length - 1, line_axis, keepdims=False),
            lax.index_in_dim(weight_low, 0, line_axis, keepdims=False),
            lax.index_in_dim(weight_low, length - 1, line_axis, keepdims=False),
            lax.index_in_dim(weight_high, 0, line_axis, keepdims=False),
            lax.index_in_dim(weight_high, length - 1, line_axis, keepdims=False),
        ]
    )[None]
    return (interior, weight_low, weight_high, edges)


def assemble(interior, weight_low, weight_high, gathered, position, line_axis):
    blocks = gathered.shape[0]
    zeros = jnp.zeros(gathered.shape[2:], jnp.float32)

    def forward(carry, block):
        ratio_prev, last_prev = carry
        first_low = -block[2]
        last_low = -block[3]
        first_high = -block[4]
        last_high = -block[5]
        pivot = 1.0 - first_low * ratio_prev
        factor_first = first_high / pivot
        factor_last = last_high + last_low * ratio_prev * factor_first
        value_first = (block[0] - first_low * last_prev) / pivot
        value_last = last_low * ratio_prev * value_first + block[1] - last_low * last_prev
        return ((factor_last, value_last), (factor_first, factor_last, value_first, value_last))

    _, factors = lax.scan(forward, (zeros, zeros), gathered)

    def backward(first_next, block):
        first_here = block[2] - block[0] * first_next
        last_here = block[3] - block[1] * first_next
        return (first_here, (first_here, last_here))

    _, (firsts, lasts) = lax.scan(backward, zeros, factors, reverse=True)
    last_before = lax.dynamic_index_in_dim(
        lasts, jnp.maximum(position - 1, 0), 0, keepdims=False
    ) * (position > 0).astype(jnp.float32)
    first_after = lax.dynamic_index_in_dim(
        firsts, jnp.minimum(position + 1, blocks - 1), 0, keepdims=False
    ) * (position < blocks - 1).astype(jnp.float32)
    return (
        interior
        + weight_low * jnp.expand_dims(last_before, line_axis)
        + weight_high * jnp.expand_dims(first_after, line_axis)
    )


def per_device(salinity, zone_ids, flow_speed, fixed_cells, dispersivity):
    long_coupling, trans_coupling = couplings(zone_ids, flow_speed, fixed_cells, dispersivity)
    first = line_solve(long_coupling, salinity, 2)
    field = lax.all_to_all(first, "col", split_axis=2, concat_axis=1, tiled=True)
    coupling = lax.all_to_all(trans_coupling, "col", split_axis=2, concat_axis=1, tiled=True)
    interior, weight_low, weight_high, edges = block_parts(field, coupling, 1)
    gathered = lax.all_gather(edges, "grp", axis=0, tiled=True)
    second = assemble(interior, weight_low, weight_high, gathered, lax.axis_index("grp"), 1)
    whole_field, whole_coupling = (
        lax.all_gather(second, "lay", axis=0, tiled=True),
        lax.all_gather(coupling, "lay", axis=0, tiled=True),
    )
    solved = line_solve(whole_coupling, whole_field, 0)
    start = lax.axis_index("lay") * second.shape[0]
    return lax.dynamic_slice_in_dim(solved, start, second.shape[0], 0)


def solution(mesh):
    placed = (
        P("lay", ("grp", "col"), None),
        P("lay", ("grp", "col"), None),
        P("lay", ("grp", "col"), None),
        P("lay", ("grp", "col"), None),
        P(),
    )
    return jax.shard_map(
        per_device, mesh=mesh, in_specs=placed, out_specs=P("lay", "grp", "col"), check_vma=False
    )
```

profile of v0, /device:TPU:1, one launch (start us, length us, event | category | flops | bytes accessed | tf_op | source)
XLA Modules:
  0.0 267.7 jit_solution(5317091718694986826)
XLA Ops:
  6.5 2.0 fusion.24
  8.5 7.0 %multiply_add_fusion.8 = (f32[4,16,2048]{2,1,0:T(8,128)S(1)}, f32[4,16,2048]{2,1,0:T(8,128)S(1)}, pred[4,16,2048]{2,1,0:T(8,128)(4,1)S(1)}, pred[4,16,2048]{2,1,...) fusion(f32[4,16,2048]{2,1,0:T(8,128)} %param.17, ...), kind=kLoop, calls=%fused_computation.82 | loop fusion | flops 2883584 | bytes 3670048 | tf_op jit(solution)/shard_map/add | solution.py:46
  15.6 5.5 %multiply_multiply_fusion.1 = f32[4,16,2048]{2,1,0:T(8,128)S(1)} fusion(f32[4,16,2048]{2,1,0:T(8,128)S(1)} %copy-done.2, pred[4,16,2048]{2,1,0:T(8,128)(4,1)S(1)} %get-tuple-element.469, pred[4,16,2048]{2,1,0:T(8,128)(4,1)S(1)} %get-tuple-element.468, pred[4,16,2048]{2,1,0:T(8,128)(4,1)S(1)} %get-tuple-element.467, ...), kind=kLoop, calls=%fused_computation.85 | loop fusion | flops 1572864 | bytes 2621472 | tf_op jit(solution)/shard_map/mul | solution.py:57
  21.1 3.0 %copy.57 = f32[4,16,2048]{1,0,2:T(4,128)} copy(f32[4,16,2048]{2,1,0:T(8,128)S(1)} %multiply_multiply_fusion.1) | data formatting | bytes 1048576 | tf_op jit(solution)/shard_map/mul | solution.py:57
  24.1 5.4 %reshape.35 = f32[16,1,8192]{2,1,0:T(1,128)} reshape(f32[2048,4,16]{2,1,0:T(4,128)} %bitcast.161) | data formatting | bytes 1048576
  29.5 7.5 %all-to-all-start = ((f32[16,1,8192]{2,1,0:T(1,128)}), f32[16,1,8192]{2,1,0:T(1,128)S(1)}, u32[]{:S(2)}, u32[]{:S(2)}) async-start(f32[16,1,8192]{2,1,0:T(1,128)} %reshape.35), calls=%async_computation | async-start | bytes 1048576 | tf_op jit(solution)/shard_map/all_to_all | solution.py:127
  37.1 22.1 %while.94 = (s32[]{:T(128)}, f32[4,16,2048]{2,1,0:T(8,128)S(1)}, f32[4,16,2048]{2,1,0:T(8,128)S(1)}, f32[4,16,2048]{2,1,0:T(8,128)S(1)}, f32[4,16,2048]{2,1,0:T(...) while((s32[]{:T(128)}, f32[4,16,2048]{2,1,0:T(8,128)S(1)}, ...), condition=%wide.region_1.2_spmd, body=%wide.region_0.1_spmd.sunk | while | flops 4980748 | bytes 18874640 | solution.py:39
  54.0 1.2 dynamic-slice_multiply_fusion.10
  59.4 3.0 %copy.59 = f32[4,16,2048]{1,0,2:T(4,128)} copy(f32[4,16,2048]{2,1,0:T(8,128)S(1)} %div.38) | data formatting | bytes 1048576 | tf_op jit(solution)/shard_map/div | solution.py:42
  62.4 5.4 %reshape.37 = f32[16,1,8192]{2,1,0:T(1,128)} reshape(f32[2048,4,16]{2,1,0:T(4,128)} %bitcast.162) | data formatting | bytes 1048576
  67.8 5.7 %all-to-all-start.1 = ((f32[16,1,8192]{2,1,0:T(1,128)}), f32[16,1,8192]{2,1,0:T(1,128)S(1)}, u32[]{:S(2)}, u32[]{:S(2)}) async-start(f32[16,1,8192]{2,1,0:T(1,128)} %reshape.37), calls=%async_computation.1 | async-start | bytes 1048576 | tf_op jit(solution)/shard_map/all_to_all | solution.py:126
  74.3 1.9 reduce
  76.2 4.2 %reshape.36 = f32[2048,4,16]{2,1,0:T(4,128)} reshape(f32[16,8192]{1,0:T(8,128)S(1)} %reduce) | data formatting | bytes 1048576
  80.4 4.4 %copy.58 = f32[4,16,16,128]{3,2,1,0:T(8,128)} copy(f32[4,16,16,128]{2,0,3,1:T(4,128)} %bitcast.163) | data formatting | bytes 1048576 | tf_op jit(solution)/shard_map/all_to_all | solution.py:127
  87.0 1.9 reduce.1
  88.9 4.2 %reshape.38 = f32[2048,4,16]{2,1,0:T(4,128)} reshape(f32[16,8192]{1,0:T(8,128)S(1)} %reduce.1) | data formatting | bytes 1048576
  93.2 4.5 %copy.60 = f32[4,16,16,128]{3,2,1,0:T(8,128)} copy(f32[4,16,16,128]{2,0,3,1:T(4,128)} %bitcast.164) | data formatting | bytes 1048576 | tf_op jit(solution)/shard_map/all_to_all | solution.py:126
  98.8 25.8 %while.95 = (s32[]{:T(128)}, f32[4,256,128]{2,1,0:T(8,128)S(1)}, f32[4,256,128]{2,1,0:T(8,128)S(1)}, f32[4,256,128]{2,1,0:T(8,128)S(1)}, f32[3,4,256,128]{3,2,1,...) while((s32[]{:T(128)}, f32[4,256,128]{2,1,0:T(8,128)S(1)}, ...), condition=%wide.region_3.4_spmd, body=%wide.region_2.3_spmd.sunk | while | flops 7602188 | bytes 33554724 | solution.py:39
  100.6 1.3 multiply_add_fusion.13
  103.8 1.3 multiply_add_fusion.13
  107.0 1.3 multiply_add_fusion.13
  110.2 1.3 multiply_add_fusion.13
  113.3 1.4 multiply_add_fusion.13
  116.6 1.3 multiply_add_fusion.13
  119.9 1.3 multiply_add_fusion.13
  123.1 1.3 multiply_add_fusion.13
  126.3 13.8 %all-gather = f32[24,4,128]{2,1,0:T(4,128)S(1)} all-gather(f32[6,4,128]{2,1,0:T(4,128)S(1)} %constant_dynamic-update-slice_fusion.4), channel_id=2, replica_groups=mesh['grp'=4,'col'=16,'lay'=4] {'grp'}, dimensions={0}, use_global_device_ids=true | all-gather | bytes 61440 | tf_op jit(solution)/shard_map/all_gather | solution.py:129
  141.7 3.4 %multiply_add_fusion.6 = (f32[16,256,128]{2,1,0:T(8,128)}, f32[16,256,128]{2,1,0:T(8,128)S(1)}) fusion(f32[16,256,128]{2,1,0:T(8,128)} %all-gather.4.cloned.1.call-done), kind=kLoop, calls=%fused_computation.72 | loop fusion | flops 1572864 | bytes 6291456 | tf_op jit(solution)/shard_map/add | solution.py:46
  145.1 1.3 copy.148
  146.5 30.4 %all-gather.6.cloned.1.call-done = f32[16,256,128]{2,1,0:T(8,128)} async-done(((f32[4,256,128]{2,1,0:T(8,128)}), f32[16,256,128]{2,1,0:T(8,128)}) %all-gather.6.cloned.1.call-update) | async-done | bytes 2097168 | tf_op jit(solution)/shard_map/all_gather | solution.py:132
  176.9 81.9 %while.96 = (s32[]{:T(128)}, f32[16,256,128]{2,1,0:T(8,128)S(1)}, f32[16,256,128]{2,1,0:T(8,128)}, f32[16,256,128]{2,1,0:T(8,128)}, f32[16,256,128]{2,1,0:T(8,12...) while((s32[]{:T(128)}, f32[16,256,128]{2,1,0:T(8,128)S(1)}, ...), condition=%wide.region_9.10_spmd, body=%wide.region_8.9_spmd.sunk | while | flops 19922956 | bytes 83886376 | solution.py:39
  177.1 1.4 copy-done
  179.3 1.5 broadcast.149
  180.8 7.8 %pad_maximum_fusion.29 = (f32[48,256,128]{2,1,0:T(8,128)S(1)}, f32[48,256,128]{2,1,0:T(8,128)}, f32[48,256,128]{2,1,0:T(8,128)}) fusion(f32[16,256,128]{2,1,0:T(8,128)} %broadcast.149, f32[16,256,128]{2,1,0:T(8,128)} %get-tuple-element.970, f32[16,256,128]{2,1,0:T(8,128)} %get-tuple-element.969, f32[16,256,128]{2,1,0:T(8,128)S(1)} %get-tuple-element.967), kind=kLoop, calls=%fused_computation.25.clone.1 | loop fusion | flops 9437184 | bytes 27262976 | tf_op jit(solution)/shard_map/while/body/eval_jaxpr/concatenate | solution.py:13
  188.6 8.8 %dynamic-slice_multiply_fusion.13 = (f32[16,256,128]{2,1,0:T(8,128)}, f32[16,256,128]{2,1,0:T(8,128)}, f32[16,256,128]{2,1,0:T(8,128)S(1)}, f32[16,256,128]{2,1,0:T(8,128)}) fusion(f32[48,256,128]{2,1,0:T(8,128)} %get-tuple-element.758, s32[]{:T(128)S(6)} %select_n.145, f32[48,256,128]{2,1,0:T(8,128)S(1)} %pad_maximum_fusion.30, ...), kind=kLoop, calls=%fused_computation.33.clone.1 | loop fusion | flops 7340032 | bytes 33554440 | tf_op jit(solution)/shard_map/while/body/eval_jaxpr/mul | solution.py:26
  197.6 1.4 copy-done
  199.8 1.5 broadcast.149
  201.3 7.8 %pad_maximum_fusion.29 = (f32[48,256,128]{2,1,0:T(8,128)S(1)}, f32[48,256,128]{2,1,0:T(8,128)}, f32[48,256,128]{2,1,0:T(8,128)}) fusion(f32[16,256,128]{2,1,0:T(8,128)} %broadcast.149, f32[16,256,128]{2,1,0:T(8,128)} %get-tuple-element.970, f32[16,256,128]{2,1,0:T(8,128)} %get-tuple-element.969, f32[16,256,128]{2,1,0:T(8,128)S(1)} %get-tuple-element.967), kind=kLoop, calls=%fused_computation.25.clone.1 | loop fusion | flops 9437184 | bytes 27262976 | tf_op jit(solution)/shard_map/while/body/eval_jaxpr/concatenate | solution.py:13
  209.1 8.8 %dynamic-slice_multiply_fusion.13 = (f32[16,256,128]{2,1,0:T(8,128)}, f32[16,256,128]{2,1,0:T(8,128)}, f32[16,256,128]{2,1,0:T(8,128)S(1)}, f32[16,256,128]{2,1,0:T(8,128)}) fusion(f32[48,256,128]{2,1,0:T(8,128)} %get-tuple-element.758, s32[]{:T(128)S(6)} %select_n.145, f32[48,256,128]{2,1,0:T(8,128)S(1)} %pad_maximum_fusion.30, ...), kind=kLoop, calls=%fused_computation.33.clone.1 | loop fusion | flops 7340032 | bytes 33554440 | tf_op jit(solution)/shard_map/while/body/eval_jaxpr/mul | solution.py:26
  218.1 1.4 copy-done
  220.3 1.5 broadcast.149
  221.8 7.8 %pad_maximum_fusion.29 = (f32[48,256,128]{2,1,0:T(8,128)S(1)}, f32[48,256,128]{2,1,0:T(8,128)}, f32[48,256,128]{2,1,0:T(8,128)}) fusion(f32[16,256,128]{2,1,0:T(8,128)} %broadcast.149, f32[16,256,128]{2,1,0:T(8,128)} %get-tuple-element.970, f32[16,256,128]{2,1,0:T(8,128)} %get-tuple-element.969, f32[16,256,128]{2,1,0:T(8,128)S(1)} %get-tuple-element.967), kind=kLoop, calls=%fused_computation.25.clone.1 | loop fusion | flops 9437184 | bytes 27262976 | tf_op jit(solution)/shard_map/while/body/eval_jaxpr/concatenate | solution.py:13
  229.6 8.7 %dynamic-slice_multiply_fusion.13 = (f32[16,256,128]{2,1,0:T(8,128)}, f32[16,256,128]{2,1,0:T(8,128)}, f32[16,256,128]{2,1,0:T(8,128)S(1)}, f32[16,256,128]{2,1,0:T(8,128)}) fusion(f32[48,256,128]{2,1,0:T(8,128)} %get-tuple-element.758, s32[]{:T(128)S(6)} %select_n.145, f32[48,256,128]{2,1,0:T(8,128)S(1)} %pad_maximum_fusion.30, ...), kind=kLoop, calls=%fused_computation.33.clone.1 | loop fusion | flops 7340032 | bytes 33554440 | tf_op jit(solution)/shard_map/while/body/eval_jaxpr/mul | solution.py:26
  238.5 1.4 copy-done
  240.6 1.5 broadcast.149
  242.1 7.8 %pad_maximum_fusion.29 = (f32[48,256,128]{2,1,0:T(8,128)S(1)}, f32[48,256,128]{2,1,0:T(8,128)}, f32[48,256,128]{2,1,0:T(8,128)}) fusion(f32[16,256,128]{2,1,0:T(8,128)} %broadcast.149, f32[16,256,128]{2,1,0:T(8,128)} %get-tuple-element.970, f32[16,256,128]{2,1,0:T(8,128)} %get-tuple-element.969, f32[16,256,128]{2,1,0:T(8,128)S(1)} %get-tuple-element.967), kind=kLoop, calls=%fused_computation.25.clone.1 | loop fusion | flops 9437184 | bytes 27262976 | tf_op jit(solution)/shard_map/while/body/eval_jaxpr/concatenate | solution.py:13
  249.9 8.8 %dynamic-slice_multiply_fusion.13 = (f32[16,256,128]{2,1,0:T(8,128)}, f32[16,256,128]{2,1,0:T(8,128)}, f32[16,256,128]{2,1,0:T(8,128)S(1)}, f32[16,256,128]{2,1,0:T(8,128)}) fusion(f32[48,256,128]{2,1,0:T(8,128)} %get-tuple-element.758, s32[]{:T(128)S(6)} %select_n.145, f32[48,256,128]{2,1,0:T(8,128)S(1)} %pad_maximum_fusion.30, ...), kind=kLoop, calls=%fused_computation.33.clone.1 | loop fusion | flops 7340032 | bytes 33554440 | tf_op jit(solution)/shard_map/while/body/eval_jaxpr/mul | solution.py:26
  258.8 2.1 dynamic-slice_divide_fusion.6
  (178 shorter events, 45.9 us)
Async XLA Ops:
  6.5 9.0 %copy-start.2 = (f32[4,16,2048]{2,1,0:T(8,128)S(1)}, f32[4,16,2048]{2,1,0:T(8,128)}, u32[]{:S(2)}) copy-start(f32[4,16,2048]{2,1,0:T(8,128)} %param.17) | copy-start | bytes 1572868
  6.5 9.0 %copy-start.3 = (s32[4,16,2048]{2,1,0:T(8,128)S(1)}, s32[4,16,2048]{2,1,0:T(8,128)}, u32[]{:S(2)}) copy-start(s32[4,16,2048]{2,1,0:T(8,128)} %param.18) | copy-start | bytes 1572868
  29.5 7.6 %copy-start.1 = (f32[4,16,2048]{2,1,0:T(8,128)S(1)}, f32[4,16,2048]{2,1,0:T(8,128)}, u32[]{:S(2)}) copy-start(f32[4,16,2048]{2,1,0:T(8,128)} %param.15) | copy-start | bytes 1572868
  29.5 38.3 %all-to-all-start = ((f32[16,1,8192]{2,1,0:T(1,128)}), f32[16,1,8192]{2,1,0:T(1,128)S(1)}, u32[]{:S(2)}, u32[]{:S(2)}) async-start(f32[16,1,8192]{2,1,0:T(1,128)} %reshape.35), calls=%async_computation | async-start | bytes 1048576 | tf_op jit(solution)/shard_map/all_to_all | solution.py:127
  67.8 19.2 %all-to-all-start.1 = ((f32[16,1,8192]{2,1,0:T(1,128)}), f32[16,1,8192]{2,1,0:T(1,128)S(1)}, u32[]{:S(2)}, u32[]{:S(2)}) async-start(f32[16,1,8192]{2,1,0:T(1,128)} %reshape.37), calls=%async_computation.1 | async-start | bytes 1048576 | tf_op jit(solution)/shard_map/all_to_all | solution.py:126
  73.6 68.2 %all-gather.4.cloned.1.call-start = ((), (), s32[]{:S(2)}) async-start(), calls=%async_computation.2 | async-start | bytes 2621440 | tf_op jit(solution)/shard_map/all_gather | solution.py:133
  84.9 92.0 %all-gather.6.cloned.1.call-start = ((), (), s32[]{:S(2)}) async-start(), calls=%async_computation.3 | async-start | bytes 2621440 | tf_op jit(solution)/shard_map/all_gather | solution.py:132
  97.6 1.1 copy-start.4
  176.9 1.6 copy-start
  197.4 1.6 copy-start
  217.9 1.6 copy-start
  238.3 1.6 copy-start
Sparse Core Ops, SparseCore 0:
  85.0 35.0 all-gather.3
  141.8 35.0 all-gather.5
where the time goes:
time: 269 us; the launch traced here: 268 us
  other arithmetic  138 us (51%)
  local copies, waits for them, and re-layouts  56.2 us (21%)
  waiting for transfers between devices  30.5 us (11%)
  blocking collectives  13.8 us (5%)
  between operations  13.7 us (5%)
  starting transfers between devices  13.5 us (5%)
    mul x23, other arithmetic, one_level(): above_next = weight_above * shifted(above_now, stride, line_axis, 0.0, 1)  51.2 us
    concatenate x35, other arithmetic, shifted(): padded = jnp.concatenate([padding, values, padding], axis=line_axis)  47.4 us
    all_gather x1, waiting for transfers between devices, per_device(): lax.all_gather(second, 'lay', axis=0, tiled=True)  30.4 us
    unnamed x20, local copies, waits for them, and re-layouts  21.7 us
    all_gather x1, blocking collectives, per_device(): gathered = lax.all_gather(edges, 'grp', axis=0, tiled=True)  13.8 us
    add x8, other arithmetic, one_level(): right_now + weight_below * shifted(right_now, stride, line_axis, 0.0, -1)  10.8 us
    add x2, other arithmetic, line_solve(): 1.0 + 2.0 * coupling  10.4 us
    another operation x60, local copies, waits for them, and re-layouts  9.29 us
  transfers between devices with their start and end apart: 4, of which 1 were waited for; matrix products, arithmetic and copies ran while one was open for 32% of the time, Pallas kernels for 0%

commit v1 on v0

--- a/solution.py
+++ b/solution.py
@@ -124,7 +124,12 @@
     long_coupling, trans_coupling = couplings(zone_ids, flow_speed, fixed_cells, dispersivity)
     first = line_solve(long_coupling, salinity, 2)
     field = lax.all_to_all(first, "col", split_axis=2, concat_axis=1, tiled=True)
-    coupling = lax.all_to_all(trans_coupling, "col", split_axis=2, concat_axis=1, tiled=True)
+    coupling = jnp.concatenate(
+        lax.all_to_all(
+            jnp.stack(jnp.split(trans_coupling, lax.axis_size("col"), axis=2)), "col", 0, 0
+        ),
+        axis=1,
+    )
     interior, weight_low, weight_high, edges = block_parts(field, coupling, 1)
     gathered = lax.all_gather(edges, "grp", axis=0, tiled=True)
     second = assemble(interior, weight_low, weight_high, gathered, lax.axis_index("grp"), 1)

time: 269 us -> 265 us (0.985)
  local copies, waits for them, and re-layouts: 56.2 us -> 49.1 us
  waiting for transfers between devices: 30.5 us -> 35.7 us
    all_to_all x1, waiting for transfers between devices: 0.01 us -> 6.68 us  [per_device(): lax.all_to_all(first, 'col', split_axis=2, concat_axis=1, tiled=True)]
    all_to_all x2 -> x0, local copies, waits for them, and re-layouts: 5.03 us -> none  [per_device(): lax.all_to_all(trans_coupling, 'col', split_axis=2, concat_axis=1, tiled=...]
    mul x1 -> x0, local copies, waits for them, and re-layouts: 3.04 us -> none  [couplings(): return (opened * longit * flow_speed, opened * transv * flow_speed)]
    unnamed x20 -> x31, local copies, waits for them, and re-layouts: 21.7 us -> 20.5 us
    another operation x60 -> x61, local copies, waits for them, and re-layouts: 9.29 us -> 10 us
  transfers between devices with their start and end apart: 4 -> 4, of which waited for: 1 -> 2; matrix products, arithmetic and copies ran while one was open for 32% -> 30% of each run, Pallas kernels for 0% -> 0%
where the time goes in v1:
time: 265 us
  other arithmetic  137 us (52%)
  local copies, waits for them, and re-layouts  49.1 us (19%)
  waiting for transfers between devices  35.7 us (13%)
  blocking collectives  13.8 us (5%)
  between operations  13.7 us (5%)
  starting transfers between devices  13.3 us (5%)
    mul x23, other arithmetic, one_level(): above_next = weight_above * shifted(above_now, stride, line_axis, 0.0, 1)  51.3 us
    concatenate x35, other arithmetic, shifted(): padded = jnp.concatenate([padding, values, padding], axis=line_axis)  47.3 us
    all_gather x1, waiting for transfers between devices, per_device(): lax.all_gather(second, 'lay', axis=0, tiled=True)  29 us
    unnamed x31, local copies, waits for them, and re-layouts  20.5 us
    all_gather x1, blocking collectives, per_device(): gathered = lax.all_gather(edges, 'grp', axis=0, tiled=True)  13.8 us
    add x8, other arithmetic, one_level(): right_now + weight_below * shifted(right_now, stride, line_axis, 0.0, -1)  10.8 us
    add x2, other arithmetic, line_solve(): 1.0 + 2.0 * coupling  10.5 us
    another operation x60, local copies, waits for them, and re-layouts  9.39 us
  transfers between devices with their start and end apart: 4, of which 2 were waited for; matrix products, arithmetic and copies ran while one was open for 30% of the time, Pallas kernels for 0%

profile of v1, /device:TPU:1, one launch (start us, length us, event | category | flops | bytes accessed | tf_op | source)
XLA Modules:
  0.0 264.5 jit_solution(14287817854759553233)
XLA Ops:
  6.5 2.0 fusion.24
  8.5 7.1 %multiply_add_fusion.8 = (f32[4,16,2048]{2,1,0:T(8,128)S(1)}, f32[4,16,2048]{2,1,0:T(8,128)S(1)}, pred[4,16,2048]{2,1,0:T(8,128)(4,1)S(1)}, pred[4,16,2048]{2,1,...) fusion(f32[4,16,2048]{2,1,0:T(8,128)} %param.17, ...), kind=kLoop, calls=%fused_computation.82 | loop fusion | flops 2883584 | bytes 3670048 | tf_op jit(solution)/shard_map/add | solution.py:46
  15.6 5.4 %multiply_multiply_fusion.1 = f32[4,16,2048]{2,1,0:T(8,128)S(1)} fusion(f32[4,16,2048]{2,1,0:T(8,128)S(1)} %copy-done.2, pred[4,16,2048]{2,1,0:T(8,128)(4,1)S(1)} %get-tuple-element.463, pred[4,16,2048]{2,1,0:T(8,128)(4,1)S(1)} %get-tuple-element.462, pred[4,16,2048]{2,1,0:T(8,128)(4,1)S(1)} %get-tuple-element.461, ...), kind=kLoop, calls=%fused_computation.85 | loop fusion | flops 1572864 | bytes 2621472 | tf_op jit(solution)/shard_map/mul | solution.py:57
  30.9 7.3 %all-to-all-start = ((f32[16,4,16,128]{3,2,1,0:T(8,128)}), f32[16,4,16,128]{3,2,1,0:T(8,128)S(1)}, u32[]{:S(2)}, u32[]{:S(2)}) async-start(f32[16,4,16,128]{3,2,1,0:T(8,128)} %constant_dynamic-update-slice_fusion.4), calls=%async_computation | async-start | bytes 1048576 | tf_op jit(solution)/shard_map/all_to_all | solution.py:128
  38.4 22.1 %while.94 = (s32[]{:T(128)}, f32[4,16,2048]{2,1,0:T(8,128)S(1)}, f32[4,16,2048]{2,1,0:T(8,128)S(1)}, f32[4,16,2048]{2,1,0:T(8,128)S(1)}, f32[4,16,2048]{2,1,0:T(...) while((s32[]{:T(128)}, f32[4,16,2048]{2,1,0:T(8,128)S(1)}, ...), condition=%wide.region_1.2_spmd, body=%wide.region_0.1_spmd.sunk | while | flops 4980748 | bytes 18874640 | solution.py:39
  39.2 1.2 dynamic-slice_multiply_fusion.10
  41.2 1.2 dynamic-slice_multiply_fusion.10
  43.2 1.2 dynamic-slice_multiply_fusion.10
  53.2 1.2 dynamic-slice_multiply_fusion.10
  55.3 1.2 dynamic-slice_multiply_fusion.10
  60.6 3.1 %copy.21 = f32[4,16,2048]{1,0,2:T(4,128)} copy(f32[4,16,2048]{2,1,0:T(8,128)S(1)} %div.38) | data formatting | bytes 1048576 | tf_op jit(solution)/shard_map/div | solution.py:42
  63.7 5.4 %reshape.43 = f32[16,1,8192]{2,1,0:T(1,128)} reshape(f32[2048,4,16]{2,1,0:T(4,128)} %bitcast.221) | data formatting | bytes 1048576
  69.1 5.7 %all-to-all-start.1 = ((f32[16,1,8192]{2,1,0:T(1,128)}), f32[16,1,8192]{2,1,0:T(1,128)S(1)}, u32[]{:S(2)}, u32[]{:S(2)}) async-start(f32[16,1,8192]{2,1,0:T(1,128)} %reshape.43), calls=%async_computation.1 | async-start | bytes 1048576 | tf_op jit(solution)/shard_map/all_to_all | solution.py:126
  77.9 6.7 %all-to-all-done.1 = f32[16,1,8192]{2,1,0:T(1,128)S(1)} async-done(((f32[16,1,8192]{2,1,0:T(1,128)}), f32[16,1,8192]{2,1,0:T(1,128)S(1)}, u32[]{:S(2)}, u32[]{:S(2)}) %all-to-all-start.1) | async-done | bytes 524320 | tf_op jit(solution)/shard_map/all_to_all | solution.py:126
  85.1 1.8 reduce
  86.9 4.3 %reshape.44 = f32[2048,4,16]{2,1,0:T(4,128)} reshape(f32[16,8192]{1,0:T(8,128)S(1)} %reduce) | data formatting | bytes 1048576
  91.2 4.5 %copy.22 = f32[4,16,16,128]{3,2,1,0:T(8,128)} copy(f32[4,16,16,128]{2,0,3,1:T(4,128)} %bitcast.222) | data formatting | bytes 1048576 | tf_op jit(solution)/shard_map/all_to_all | solution.py:126
  97.1 25.8 %while.95 = (s32[]{:T(128)}, f32[4,256,128]{2,1,0:T(8,128)S(1)}, f32[4,256,128]{2,1,0:T(8,128)S(1)}, f32[4,256,128]{2,1,0:T(8,128)S(1)}, f32[3,4,256,128]{3,2,1,...) while((s32[]{:T(128)}, f32[4,256,128]{2,1,0:T(8,128)S(1)}, ...), condition=%wide.region_3.4_spmd, body=%wide.region_2.3_spmd.sunk | while | flops 7602188 | bytes 33554724 | solution.py:39
  98.9 1.3 multiply_add_fusion.13
  102.1 1.3 multiply_add_fusion.13
  105.3 1.3 multiply_add_fusion.13
  108.5 1.3 multiply_add_fusion.13
  111.6 1.4 multiply_add_fusion.13
  114.9 1.3 multiply_add_fusion.13
  118.2 1.3 multiply_add_fusion.13
  121.4 1.3 multiply_add_fusion.13
  124.6 13.8 %all-gather = f32[24,4,128]{2,1,0:T(4,128)S(1)} all-gather(f32[6,4,128]{2,1,0:T(4,128)S(1)} %constant_dynamic-update-slice_fusion.20), channel_id=2, replica_groups=mesh['grp'=4,'col'=16,'lay'=4] {'grp'}, dimensions={0}, use_global_device_ids=true | all-gather | bytes 61440 | tf_op jit(solution)/shard_map/all_gather | solution.py:134
  140.0 3.4 %multiply_add_fusion.6 = (f32[16,256,128]{2,1,0:T(8,128)}, f32[16,256,128]{2,1,0:T(8,128)S(1)}) fusion(f32[16,256,128]{2,1,0:T(8,128)} %all-gather.4.cloned.1.call-done), kind=kLoop, calls=%fused_computation.72 | loop fusion | flops 1572864 | bytes 6291456 | tf_op jit(solution)/shard_map/add | solution.py:46
  143.3 1.4 copy.125
  144.7 29.0 %all-gather.6.cloned.1.call-done = f32[16,256,128]{2,1,0:T(8,128)} async-done(((f32[4,256,128]{2,1,0:T(8,128)}), f32[16,256,128]{2,1,0:T(8,128)}) %all-gather.6.cloned.1.call-update) | async-done | bytes 2097168 | tf_op jit(solution)/shard_map/all_gather | solution.py:137
  173.7 81.9 %while.96 = (s32[]{:T(128)}, f32[16,256,128]{2,1,0:T(8,128)S(1)}, f32[16,256,128]{2,1,0:T(8,128)}, f32[16,256,128]{2,1,0:T(8,128)}, f32[16,256,128]{2,1,0:T(8,12...) while((s32[]{:T(128)}, f32[16,256,128]{2,1,0:T(8,128)S(1)}, ...), condition=%wide.region_9.10_spmd, body=%wide.region_8.9_spmd.sunk | while | flops 19922956 | bytes 83886376 | solution.py:39
  173.9 1.4 copy-done
  176.0 1.6 broadcast.148
  177.6 7.8 %pad_maximum_fusion.29 = (f32[48,256,128]{2,1,0:T(8,128)S(1)}, f32[48,256,128]{2,1,0:T(8,128)}, f32[48,256,128]{2,1,0:T(8,128)}) fusion(f32[16,256,128]{2,1,0:T(8,128)} %broadcast.148, f32[16,256,128]{2,1,0:T(8,128)} %get-tuple-element.964, f32[16,256,128]{2,1,0:T(8,128)} %get-tuple-element.963, f32[16,256,128]{2,1,0:T(8,128)S(1)} %get-tuple-element.961), kind=kLoop, calls=%fused_computation.25.clone.1 | loop fusion | flops 9437184 | bytes 27262976 | tf_op jit(solution)/shard_map/while/body/eval_jaxpr/concatenate | solution.py:13
  185.4 8.8 %dynamic-slice_multiply_fusion.13 = (f32[16,256,128]{2,1,0:T(8,128)}, f32[16,256,128]{2,1,0:T(8,128)}, f32[16,256,128]{2,1,0:T(8,128)S(1)}, f32[16,256,128]{2,1,0:T(8,128)}) fusion(f32[48,256,128]{2,1,0:T(8,128)} %get-tuple-element.752, s32[]{:T(128)S(6)} %select_n.145, f32[48,256,128]{2,1,0:T(8,128)S(1)} %pad_maximum_fusion.30, ...), kind=kLoop, calls=%fused_computation.33.clone.1 | loop fusion | flops 7340032 | bytes 33554440 | tf_op jit(solution)/shard_map/while/body/eval_jaxpr/mul | solution.py:26
  194.4 1.4 copy-done
  196.6 1.6 broadcast.148
  198.1 7.8 %pad_maximum_fusion.29 = (f32[48,256,128]{2,1,0:T(8,128)S(1)}, f32[48,256,128]{2,1,0:T(8,128)}, f32[48,256,128]{2,1,0:T(8,128)}) fusion(f32[16,256,128]{2,1,0:T(8,128)} %broadcast.148, f32[16,256,128]{2,1,0:T(8,128)} %get-tuple-element.964, f32[16,256,128]{2,1,0:T(8,128)} %get-tuple-element.963, f32[16,256,128]{2,1,0:T(8,128)S(1)} %get-tuple-element.961), kind=kLoop, calls=%fused_computation.25.clone.1 | loop fusion | flops 9437184 | bytes 27262976 | tf_op jit(solution)/shard_map/while/body/eval_jaxpr/concatenate | solution.py:13
  205.9 8.8 %dynamic-slice_multiply_fusion.13 = (f32[16,256,128]{2,1,0:T(8,128)}, f32[16,256,128]{2,1,0:T(8,128)}, f32[16,256,128]{2,1,0:T(8,128)S(1)}, f32[16,256,128]{2,1,0:T(8,128)}) fusion(f32[48,256,128]{2,1,0:T(8,128)} %get-tuple-element.752, s32[]{:T(128)S(6)} %select_n.145, f32[48,256,128]{2,1,0:T(8,128)S(1)} %pad_maximum_fusion.30, ...), kind=kLoop, calls=%fused_computation.33.clone.1 | loop fusion | flops 7340032 | bytes 33554440 | tf_op jit(solution)/shard_map/while/body/eval_jaxpr/mul | solution.py:26
  214.9 1.4 copy-done
  217.1 1.6 broadcast.148
  218.6 7.8 %pad_maximum_fusion.29 = (f32[48,256,128]{2,1,0:T(8,128)S(1)}, f32[48,256,128]{2,1,0:T(8,128)}, f32[48,256,128]{2,1,0:T(8,128)}) fusion(f32[16,256,128]{2,1,0:T(8,128)} %broadcast.148, f32[16,256,128]{2,1,0:T(8,128)} %get-tuple-element.964, f32[16,256,128]{2,1,0:T(8,128)} %get-tuple-element.963, f32[16,256,128]{2,1,0:T(8,128)S(1)} %get-tuple-element.961), kind=kLoop, calls=%fused_computation.25.clone.1 | loop fusion | flops 9437184 | bytes 27262976 | tf_op jit(solution)/shard_map/while/body/eval_jaxpr/concatenate | solution.py:13
  226.4 8.7 %dynamic-slice_multiply_fusion.13 = (f32[16,256,128]{2,1,0:T(8,128)}, f32[16,256,128]{2,1,0:T(8,128)}, f32[16,256,128]{2,1,0:T(8,128)S(1)}, f32[16,256,128]{2,1,0:T(8,128)}) fusion(f32[48,256,128]{2,1,0:T(8,128)} %get-tuple-element.752, s32[]{:T(128)S(6)} %select_n.145, f32[48,256,128]{2,1,0:T(8,128)S(1)} %pad_maximum_fusion.30, ...), kind=kLoop, calls=%fused_computation.33.clone.1 | loop fusion | flops 7340032 | bytes 33554440 | tf_op jit(solution)/shard_map/while/body/eval_jaxpr/mul | solution.py:26
  235.3 1.4 copy-done
  237.5 1.6 broadcast.148
  239.0 7.8 %pad_maximum_fusion.29 = (f32[48,256,128]{2,1,0:T(8,128)S(1)}, f32[48,256,128]{2,1,0:T(8,128)}, f32[48,256,128]{2,1,0:T(8,128)}) fusion(f32[16,256,128]{2,1,0:T(8,128)} %broadcast.148, f32[16,256,128]{2,1,0:T(8,128)} %get-tuple-element.964, f32[16,256,128]{2,1,0:T(8,128)} %get-tuple-element.963, f32[16,256,128]{2,1,0:T(8,128)S(1)} %get-tuple-element.961), kind=kLoop, calls=%fused_computation.25.clone.1 | loop fusion | flops 9437184 | bytes 27262976 | tf_op jit(solution)/shard_map/while/body/eval_jaxpr/concatenate | solution.py:13
  246.8 8.8 %dynamic-slice_multiply_fusion.13 = (f32[16,256,128]{2,1,0:T(8,128)}, f32[16,256,128]{2,1,0:T(8,128)}, f32[16,256,128]{2,1,0:T(8,128)S(1)}, f32[16,256,128]{2,1,0:T(8,128)}) fusion(f32[48,256,128]{2,1,0:T(8,128)} %get-tuple-element.752, s32[]{:T(128)S(6)} %select_n.145, f32[48,256,128]{2,1,0:T(8,128)S(1)} %pad_maximum_fusion.30, ...), kind=kLoop, calls=%fused_computation.33.clone.1 | loop fusion | flops 7340032 | bytes 33554440 | tf_op jit(solution)/shard_map/while/body/eval_jaxpr/mul | solution.py:26
  255.6 2.1 dynamic-slice_divide_fusion.6
  (188 shorter events, 52.1 us)
Async XLA Ops:
  6.5 9.0 %copy-start.2 = (f32[4,16,2048]{2,1,0:T(8,128)S(1)}, f32[4,16,2048]{2,1,0:T(8,128)}, u32[]{:S(2)}) copy-start(f32[4,16,2048]{2,1,0:T(8,128)} %param.17) | copy-start | bytes 1572868
  6.5 9.0 %copy-start.3 = (s32[4,16,2048]{2,1,0:T(8,128)S(1)}, s32[4,16,2048]{2,1,0:T(8,128)}, u32[]{:S(2)}) copy-start(s32[4,16,2048]{2,1,0:T(8,128)} %param.18) | copy-start | bytes 1572868
  21.0 17.4 %copy-start.1 = (f32[4,16,2048]{2,1,0:T(8,128)S(1)}, f32[4,16,2048]{2,1,0:T(8,128)}, u32[]{:S(2)}) copy-start(f32[4,16,2048]{2,1,0:T(8,128)} %param.15) | copy-start | bytes 1572868
  30.9 38.2 %all-to-all-start = ((f32[16,4,16,128]{3,2,1,0:T(8,128)}), f32[16,4,16,128]{3,2,1,0:T(8,128)S(1)}, u32[]{:S(2)}, u32[]{:S(2)}) async-start(f32[16,4,16,128]{3,2,1,0:T(8,128)} %constant_dynamic-update-slice_fusion.4), calls=%async_computation | async-start | bytes 1048576 | tf_op jit(solution)/shard_map/all_to_all | solution.py:128
  69.1 15.5 %all-to-all-start.1 = ((f32[16,1,8192]{2,1,0:T(1,128)}), f32[16,1,8192]{2,1,0:T(1,128)S(1)}, u32[]{:S(2)}, u32[]{:S(2)}) async-start(f32[16,1,8192]{2,1,0:T(1,128)} %reshape.43), calls=%async_computation.1 | async-start | bytes 1048576 | tf_op jit(solution)/shard_map/all_to_all | solution.py:126
  74.8 65.1 %all-gather.4.cloned.1.call-start = ((), (), s32[]{:S(2)}) async-start(), calls=%async_computation.2 | async-start | bytes 2621440 | tf_op jit(solution)/shard_map/all_gather | solution.py:138
  75.8 97.9 %all-gather.6.cloned.1.call-start = ((), (), s32[]{:S(2)}) async-start(), calls=%async_computation.3 | async-start | bytes 2621440 | tf_op jit(solution)/shard_map/all_gather | solution.py:137
  173.7 1.6 copy-start
  194.2 1.6 copy-start
  214.7 1.6 copy-start
  235.1 1.6 copy-start
Sparse Core Ops, SparseCore 0:
  77.5 35.0 all-gather.3
  140.0 33.5 all-gather.5
